TPU v7x, 128 devices: a whole 4x4x4 slice. The times are simulated.
128 devices in a mesh: seq: 16 (over z, x), req: 8 (over y, core).
Axes of the slice: x: 4, y: 4, z: 4, core: 2. Of those that a mesh axis runs over, the one named last changes fastest.
Arguments:
- given_token_index: int32 [128], replicated, may hold values from 0 to 31999
- hidden: bfloat16 [128, 3584], P('req'), may hold values from -6 to 6
- token_embedding_table: bfloat16 [32000, 3584], P(('seq', 'req')), may hold values from -6 to 6
- attention_norm_gain: bfloat16 [7168], replicated, may hold values from 0.099609375 to 1.8984375
- query_key_value_weight: bfloat16 [7168, 10752], P('req', 'seq'), may hold values from -0.0625 to 0.0625
- rotated_key_cache: bfloat16 [96, 8, 128, 3584], P('seq', 'req'), may hold values from -240 to 240
- cached_value_pages: bfloat16 [96, 8, 128, 3584], P('seq', 'req'), may hold values from -6 to 6
- lengths: int32 [32], P('req'), may hold values from 1 to 6144, as said below
- request_page_slots: int32 [32, 48], P('req'), may hold values from 0 to 95, as said below
- attention_output_weight: bfloat16 [3584, 7168], P('seq'), may hold values from -0.375 to 0.375
- feedforward_norm_gain: bfloat16 [7168], replicated, may hold values from 0.099609375 to 1.8984375
- gate_weight: bfloat16 [7168, 14336], P('req', 'seq'), may hold values from -0.0625 to 0.0625
- up_weight: bfloat16 [7168, 14336], P('req', 'seq'), may hold values from -0.0625 to 0.0625
- adapter_down_map: bfloat16 [7168, 128], P('req'), may hold values from -0.0625 to 0.0625
- adapter_gate_map: bfloat16 [128, 14336], P(None, 'seq'), may hold values from -0.5 to 0.5
- adapter_up_map: bfloat16 [128, 14336], P(None, 'seq'), may hold values from -0.5 to 0.5
- down_weight: bfloat16 [14336, 7168], P('seq', 'req'), may hold values from -0.046875 to 0.046875
Outputs:
- block_out: bfloat16 [128, 7168], P('seq', 'req')
Inputs may be any that keep to these rules, and one draw needn't show every extreme that they name: `lengths`: in each group of 4 requests exactly one has 6144 tokens, and the pages of a group's requests number at most 96 together. `request_page_slots`: entry p of request i names a slot of its group, 0 to 95; the entries with p * 128 below lengths[i] are distinct within a group, the others name any slot. Slot g of a group lies on the seq index g // 6, at place g % 6.
All inputs are finite; a program needn't handle non-finite values.
Results may differ from a plain program's by a relative error of at most 0.028.
The roundings to bfloat16 on the way count: a program that leaves them out, or rounds other values in their place, can miss the bound.
Values may be sent and summed in bfloat16 or wider, within the bound.
A program may use at most 128 MiB of HBM per device.

v0:
```python
import math
import jax
import jax.numpy as jnp
from jax import lax
from jax.sharding import PartitionSpec as P

HEADS = 16
HD = 224
NEGATIVE = -1e30
EPSILON = 1e-05
ROTARY_BASE = 10000.0


def merged_2(array, axis, combine):
    everything = jax.tree.map(lambda part: lax.all_gather(part, axis), array)
    first = jax.tree.map(lambda part: part[0], everything)

    def hop(k, so_far):
        return combine(so_far, jax.tree.map(lambda part: part[k], everything))

    return lax.fori_loop(1, lax.axis_size(axis), hop, first)


def rms_norm(matrix, gain_vec):
    widened = matrix.astype(jnp.float32)
    factor = lax.rsqrt(jnp.mean(widened * widened, axis=-1, keepdims=True) + EPSILON)
    return (widened * factor * gain_vec.astype(jnp.float32)).astype(jnp.bfloat16)


def rotate(vectors, positions):
    half_dim = vectors.shape[-1] // 2
    frequency = ROTARY_BASE ** (-2.0 * jnp.arange(half_dim, dtype=jnp.float32) / vectors.shape[-1])
    angles = positions.astype(jnp.float32)[..., None, None] * frequency
    cosine = jnp.cos(angles)
    sine_part = jnp.sin(angles)
    front_half = vectors[..., :half_dim]
    back_half = vectors[..., half_dim:]
    return jnp.concatenate(
        [front_half * cosine - back_half * sine_part, back_half * cosine + front_half * sine_part],
        axis=-1,
    )


def softmax_join(earlier, later):
    first_max, first_sum, first_out = earlier
    second_max, second_sum, second_out = later
    overall = jnp.maximum(first_max, second_max)
    first_factor = jnp.exp(first_max - overall)
    second_factor = jnp.exp(second_max - overall)
    return (
        overall,
        first_sum * first_factor + second_sum * second_factor,
        first_out * first_factor[..., None] + second_out * second_factor[..., None],
    )


def body(
    given_token_index,
    hidden,
    token_embedding_table,
    attention_norm_gain,
    query_key_value_weight,
    rotated_key_cache,
    cached_value_pages,
    lengths,
    request_page_slots,
    attention_output_weight,
    feedforward_norm_gain,
    gate_weight,
    up_weight,
    adapter_down_map,
    adapter_gate_map,
    adapter_up_map,
    down_weight,
):
    seq_devices = lax.axis_size("seq")
    req_devices = lax.axis_size("req")
    seq_index = lax.axis_index("seq")
    req_index = lax.axis_index("req")
    group_rows = hidden.shape[0]
    requests = lengths.shape[0]
    steps_each = group_rows // requests
    vocab_rows = token_embedding_table.shape[0]
    first_id = (seq_index * req_devices + req_index) * vocab_rows
    local_ids = given_token_index - first_id
    present = (local_ids >= 0) & (local_ids < vocab_rows)
    looked = jnp.take(token_embedding_table, jnp.clip(local_ids, 0, vocab_rows - 1), axis=0).astype(
        jnp.float32
    )
    looked = jnp.where(present[:, None], looked, 0.0)
    everywhere = lax.psum(looked, ("seq", "req"))
    embedded = lax.dynamic_slice_in_dim(everywhere, req_index * group_rows, group_rows, 0)
    joined = jnp.concatenate([hidden, embedded.astype(jnp.bfloat16)], axis=1)
    normed = rms_norm(joined, attention_norm_gain)
    spread = lax.all_to_all(normed, "req", split_axis=1, concat_axis=0, tiled=True)
    block_rows = spread
    qkv_part = lax.psum_scatter(
        jnp.dot(block_rows, query_key_value_weight, preferred_element_type=jnp.float32),
        "req",
        scatter_dimension=0,
        tiled=True,
    )
    projected = lax.all_gather(qkv_part.astype(jnp.bfloat16), "seq", axis=1, tiled=True)
    head_cols = HEADS * HD
    queries = projected[:, :head_cols].reshape(requests, steps_each, HEADS, HD)
    new_keys = projected[:, head_cols : 2 * head_cols].reshape(requests, steps_each, HEADS, HD)
    new_values = projected[:, 2 * head_cols :].reshape(requests, steps_each, HEADS, HD)
    positions = lengths[:, None] + jnp.arange(steps_each, dtype=jnp.int32)[None, :]
    queries = rotate(queries.astype(jnp.float32), positions).astype(jnp.bfloat16)
    new_keys = rotate(new_keys.astype(jnp.float32), positions).astype(jnp.bfloat16)
    slots = rotated_key_cache.shape[0]
    page_len = rotated_key_cache.shape[2]
    cache_k = rotated_key_cache.reshape(slots * page_len, HEADS, HD)
    cache_v = cached_value_pages.reshape(slots * page_len, HEADS, HD)
    slot_ids = seq_index * slots + jnp.arange(slots, dtype=jnp.int32)
    page_ids = jnp.arange(request_page_slots.shape[1], dtype=jnp.int32)
    is_live = page_ids[None, :] < ((lengths + page_len - 1) // page_len)[:, None]
    matches = (request_page_slots[:, :, None] == slot_ids[None, None, :]) & is_live[:, :, None]
    is_owned = jnp.any(matches, axis=1)
    page_of = jnp.sum(jnp.where(matches, page_ids[None, :, None], 0), axis=1)
    token_pos = (
        page_of[:, :, None] * page_len + jnp.arange(page_len, dtype=jnp.int32)[None, None, :]
    )
    is_valid = (is_owned[:, :, None] & (token_pos < lengths[:, None, None])).reshape(
        requests, slots * page_len
    )
    score_scale = 1.0 / math.sqrt(HD)
    scores = (
        jnp.einsum("rthd,khd->rthk", queries, cache_k, preferred_element_type=jnp.float32)
        * score_scale
    )
    mask_b = is_valid[:, None, None, :]
    local_max = jnp.max(jnp.where(mask_b, scores, NEGATIVE), axis=-1)
    weights = jnp.where(mask_b, jnp.exp(scores - local_max[..., None]), 0.0)
    local_sum = jnp.sum(weights, axis=-1)
    local_out = jnp.einsum(
        "rthk,khd->rthd", weights.astype(jnp.bfloat16), cache_v, preferred_element_type=jnp.float32
    )
    fresh_scores = (
        jnp.einsum("rthd,rshd->rths", queries, new_keys, preferred_element_type=jnp.float32)
        * score_scale
    )
    causal = jnp.arange(steps_each)[:, None] >= jnp.arange(steps_each)[None, :]
    fresh_mask = causal[None, :, None, :]
    fresh_max = jnp.max(jnp.where(fresh_mask, fresh_scores, NEGATIVE), axis=-1)
    fresh_w = jnp.where(fresh_mask, jnp.exp(fresh_scores - fresh_max[..., None]), 0.0)
    fresh_sum = jnp.sum(fresh_w, axis=-1)
    fresh_out = jnp.einsum(
        "rths,rshd->rthd",
        fresh_w.astype(jnp.bfloat16),
        new_values,
        preferred_element_type=jnp.float32,
    )
    own_heads = HEADS // seq_devices
    first_head = seq_index * own_heads

    def own_slice(member):
        return lax.dynamic_slice_in_dim(member, first_head, own_heads, 2)

    fresh_part = (own_slice(fresh_max), own_slice(fresh_sum), own_slice(fresh_out))
    merged = merged_2((local_max, local_sum, local_out), "seq", softmax_join)
    combined = softmax_join(tuple((own_slice(member) for member in merged)), fresh_part)
    attention = (
        (combined[2] / combined[1][..., None])
        .astype(jnp.bfloat16)
        .reshape(group_rows, own_heads * HD)
    )
    projected_out = jnp.dot(attention, attention_output_weight, preferred_element_type=jnp.float32)
    mixed_sum = lax.psum(projected_out, "seq")
    after_attn = (joined.astype(jnp.float32) + mixed_sum).astype(jnp.bfloat16)
    second_normed_state = rms_norm(after_attn, feedforward_norm_gain)
    residual_cols, second_spread_state = (
        lax.all_to_all(after_attn, "req", split_axis=1, concat_axis=0, tiled=True),
        lax.all_to_all(second_normed_state, "req", split_axis=1, concat_axis=0, tiled=True),
    )
    gate_total, up_total, low_sum = lax.psum(
        (
            jnp.dot(second_spread_state, gate_weight, preferred_element_type=jnp.float32),
            jnp.dot(second_spread_state, up_weight, preferred_element_type=jnp.float32),
            jnp.dot(second_spread_state, adapter_down_map, preferred_element_type=jnp.float32),
        ),
        "req",
    )
    adapter_hidden = low_sum.astype(jnp.bfloat16)
    gate_preactivation = gate_total + jnp.dot(
        adapter_hidden, adapter_gate_map, preferred_element_type=jnp.float32
    )
    up_projection_part = up_total + jnp.dot(
        adapter_hidden, adapter_up_map, preferred_element_type=jnp.float32
    )
    inner_act = (jax.nn.silu(gate_preactivation) * up_projection_part).astype(jnp.bfloat16)
    out_rows = residual_cols.shape[0] // seq_devices
    block_rows = inner_act
    down_sum = lax.psum_scatter(
        jnp.dot(block_rows, down_weight, preferred_element_type=jnp.float32),
        "seq",
        scatter_dimension=0,
        tiled=True,
    )
    residual_rows = lax.dynamic_slice_in_dim(residual_cols, seq_index * out_rows, out_rows, 0)
    return (residual_rows.astype(jnp.float32) + down_sum).astype(jnp.bfloat16)


def solution(mesh):
    placed = (
        P(),
        P("req", None),
        P(("seq", "req"), None),
        P(),
        P("req", "seq"),
        P("seq", "req", None, None),
        P("seq", "req", None, None),
        P("req"),
        P("req", None),
        P("seq", None),
        P(),
        P("req", "seq"),
        P("req", "seq"),
        P("req", None),
        P(None, "seq"),
        P(None, "seq"),
        P("seq", "req"),
    )
    return jax.shard_map(
        body, mesh=mesh, in_specs=placed, out_specs=P("seq", "req"), check_vma=False
    )
```

profile of v0, /device:TPU:0, one launch (start us, length us, event | category | flops | bytes accessed | tf_op | source)
XLA Modules:
  0.0 529.0 jit_solution(585776612457046075)
XLA Ops:
  7.4 4.9 gather_fusion
  12.2 2.8 convert_select_fusion
  15.0 74.1 %all-reduce.12 = bf16[128,3584]{1,0:T(8,128)(2,1)} all-reduce(f32[128,3584]{1,0:T(8,128)} %convert_select_fusion), channel_id=1, replica_groups=mesh['seq'=16,'req'=8] {'seq','req'}, use_global_device_ids=true, to_apply=%region_0.1 | all-reduce | flops 458752 | bytes 2752512 | tf_op jit(solution)/shard_map/psum | solution.py:91
  94.6 3.9 all-to-all-start
  100.2 1.5 fusion.55
  102.9 1.3 copy.111
  104.2 1.3 broadcast_bitcast_fusion.1
  105.4 1.3 add_convert_fusion.2
  106.7 2.6 fusion.67
  110.2 13.1 %reshape.185 = bf16[768,16,224]{2,1,0:T(8,128)(2,1)} reshape(bf16[6,1,128,3584]{3,2,1,0:T(8,128)(2,1)} %param.24) | data formatting | bytes 11010048 | tf_op jit(solution)/shard_map/reshape | solution.py:113
  123.3 13.2 %reshape.186 = bf16[768,16,224]{2,1,0:T(8,128)(2,1)} reshape(bf16[6,1,128,3584]{3,2,1,0:T(8,128)(2,1)} %param.25) | data formatting | bytes 11010048 | tf_op jit(solution)/shard_map/reshape | solution.py:114
  139.9 24.2 %all-gather.3 = bf16[16,672,16]{1,2,0:T(8,128)(2,1)S(1)} all-gather(bf16[1,672,16]{1,2,0:T(8,128)(2,1)S(1)} %convert_bitcast_fusion), channel_id=1, replica_groups=mesh['seq'=16,'req'=8] {'seq'}, dimensions={0}, use_global_device_ids=true | all-gather | bytes 365568 | tf_op jit(solution)/shard_map/all_gather | solution.py:103
  165.0 1.5 reshape.211
  170.6 1.3 subtract_convert_fusion
  171.9 6.8 %select_reduce_fusion = (f32[4,4,16]{1,0,2:T(4,128)S(1)}, f32[4,4,16,768]{3,1,0,2:T(4,128)S(1)}) fusion(pred[4,768]{1,0:T(4,128)(4,1)} %fusion.54, bf16[768,16,224,1]{2,1,0,3:T(8,128)(2,1)} %bitcast.116, bf16[4,4,16,112]{3,1,0,2:T(4,128)(2,1)S(1)} %get-tuple-element.268, bf16[4,4,16,112]{3,1,0,2:T(4,128)(2,1)S(1)} %get-tuple-element.269), kind=kOutput, calls=%fused_computation.25 | convolution fusion | flops 88899328 | bytes 6410240 | tf_op jit(solution)/shard_map/rthd,khd->rthk/dot_general | solution.py:129
  179.7 4.6 fusion.16
  185.6 2.3 fusion.21
  188.7 22.9 %all-gather.1 = f32[64,4,16]{2,1,0:T(4,128)S(1)} all-gather(f32[4,4,16]{2,1,0:T(4,128)S(1)} %copy.119), channel_id=3, replica_groups=mesh['seq'=16,'req'=8] {'seq'}, dimensions={0}, use_global_device_ids=true | all-gather | bytes 17408 | tf_op jit(solution)/shard_map/all_gather | solution.py:15
  211.7 21.9 %all-gather = f32[64,4,16]{2,1,0:T(4,128)S(1)} all-gather(f32[4,4,16]{2,1,0:T(4,128)} %copy.118), channel_id=2, replica_groups=mesh['seq'=16,'req'=8] {'seq'}, dimensions={0}, use_global_device_ids=true | all-gather | bytes 17408 | tf_op jit(solution)/shard_map/all_gather | solution.py:15
  242.3 29.8 %while.19 = (s32[]{:T(128)}, f32[4,4,16]{2,1,0:T(4,128)S(1)}, f32[4,4,16]{2,1,0:T(4,128)S(1)}, f32[4,4,16,224]{3,2,1,0:T(8,128)S(1)}, f32[16,4,4,16]{3,2,1,0:T(4...) while((s32[]{:T(128)}, f32[4,4,16]{2,1,0:T(4,128)S(1)}, ...), condition=%wide.region_8.9_spmd, body=%wide.region_7.8_spmd.sunk | while | flops 173573 | bytes 1157271 | solution.py:21
  274.1 1.3 fusion.68
  275.5 81.3 %all-reduce.7.cloned.1.call-done = f32[16,7168]{1,0:T(8,128)} async-done(((f32[16,7168]{1,0:T(8,128)}), f32[16,7168]{1,0:T(8,128)}) %all-reduce.7.cloned.1.call-update) | async-done | bytes 458768 | tf_op jit(solution)/shard_map/psum | solution.py:169
  356.7 1.3 fusion.24
  358.2 11.4 %all_to_all.54 = bf16[16,8,896]{2,0,1:T(8,128)(2,1)S(1)} all-to-all(bf16[16,8,896]{2,0,1:T(8,128)(2,1)S(1)} %bitcast.125), channel_id=1, replica_groups=mesh['seq'=16,'req'=8] {'req'}, dimensions={1} | all-to-all | bytes 458752 | tf_op jit(solution)/shard_map/all_to_all | solution.py:174
  373.4 24.2 %psum.38 = bf16[128,128]{1,0:T(8,128)(2,1)S(1)} all-reduce(f32[128,128]{1,0:T(8,128)S(1)} %fusion.70), channel_id=1, replica_groups=mesh['seq'=16,'req'=8] {'req'}, use_global_device_ids=true, to_apply=%region_14.15 | all-reduce | flops 16384 | bytes 98304 | tf_op jit(solution)/shard_map/psum | solution.py:176
  397.5 34.2 %all-reduce.11.cloned.1.call-done = (f32[128,896]{1,0:T(8,128)}, f32[128,896]{1,0:T(8,128)}) async-done(((f32[128,896]{1,0:T(8,128)}, f32[128,896]{1,0:T(8,128)}), (f32[128,896]{1,0:T(8,128)}, f32[128,896]{1,0:T(8,128)})) %all-reduce.11.cloned.1.call-update) | async-done | bytes 917520 | tf_op jit(solution)/shard_map/psum | solution.py:176
  431.8 2.1 convolution_add_fusion.1
  433.9 3.2 fusion.19
  437.9 3.4 all-to-all-start.1
  442.5 5.9 %all-to-all-done.1 = bf16[16,8,896]{2,0,1:T(8,128)(2,1)S(1)} async-done(((bf16[16,8,896]{2,0,1:T(8,128)(2,1)}), bf16[16,8,896]{2,0,1:T(8,128)(2,1)S(1)}, u32[]{:S(2)}, u32[]{:S(2)}) %all-to-all-start.1) | async-done | bytes 229408 | tf_op jit(solution)/shard_map/all_to_all | solution.py:173
  448.4 72.7 %all-reduce.9.cloned.1.call-done = f32[128,896]{1,0:T(8,128)} async-done(((f32[128,896]{1,0:T(8,128)}), f32[128,896]{1,0:T(8,128)}) %all-reduce.9.cloned.1.call-update) | async-done | bytes 458768
  521.1 1.4 fusion.45
  (171 shorter events, 66.6 us)
Async XLA Ops:
  6.5 267.5 %copy-start = (bf16[224,7168]{1,0:T(8,128)(2,1)S(1)}, bf16[224,7168]{1,0:T(8,128)(2,1)}, u32[]{:S(2)}) copy-start(bf16[224,7168]{1,0:T(8,128)(2,1)} %param.28) | copy-start | bytes 9633796
  15.0 75.1 %copy-start.7 = (bf16[16,3584]{1,0:T(8,128)(2,1)S(1)}, bf16[16,3584]{1,0:T(8,128)(2,1)}, u32[]{:S(2)}) copy-start(bf16[16,3584]{1,0:T(8,128)(2,1)} %param.20) | copy-start | bytes 344068
  90.0 19.3 %copy-start.3 = (bf16[16,3584]{1,0:T(8,128)(2,1)}, bf16[16,3584]{1,0:T(8,128)(2,1)S(1)}, u32[]{:S(2)}) copy-start(bf16[16,3584]{1,0:T(8,128)(2,1)S(1)} %dynamic-slice_convert_fusion) | copy-start | bytes 344068
  94.6 12.1 %all-to-all-start = ((bf16[16,8,896]{2,0,1:T(8,128)(2,1)}), bf16[16,8,896]{2,0,1:T(8,128)(2,1)S(1)}, u32[]{:S(2)}, u32[]{:S(2)}) async-start(bf16[16,8,896]{2,0,1:T(8,128)(2,1)} %copy.113), calls=%async_computation | async-start | bytes 458752 | tf_op jit(solution)/shard_map/all_to_all | solution.py:95
  98.5 40.6 %reduce-scatter.2.cloned.1.call-start = ((), (), s32[]{:S(2)}) async-start(), calls=%async_computation.4 | async-start | bytes 442368 | tf_op jit(solution)/shard_map/reduce_scatter | solution.py:97
  109.3 131.8 %all-gather.6.cloned.1.call-start = ((), (), s32[]{:S(2)}) async-start(), calls=%async_computation.6 | async-start | bytes 4456448 | tf_op jit(solution)/shard_map/all_gather | solution.py:15
  123.3 13.2 %copy-start.20 = (f32[4,4]{1,0:T(4,128)S(1)}, f32[4,4]{1,0:T(4,128)}, u32[]{:S(2)}) copy-start(f32[4,4]{1,0:T(4,128)} %add_convert_fusion.2) | copy-start | bytes 196
  123.3 14.0 %copy-start.16 = (s32[768]{0:T(1024)S(1)}, s32[768]{0:T(1024)}, u32[]{:S(2)}) copy-start(s32[768]{0:T(1024)} %iota_bitcast_fusion) | copy-start | bytes 9220
  123.3 14.0 %copy-start.17 = (pred[1,4,6,128]{3,2,1,0:T(8,128)(4,1)S(1)}, pred[1,4,6,128]{3,2,1,0:T(8,128)(4,1)}, u32[]{:S(2)}) copy-start(pred[1,4,6,128]{3,2,1,0:T(8,128)(4,1)} %broadcast_bitcast_fusion.1) | copy-start | bytes 9220
  123.3 14.0 %copy-start.21 = (s32[4]{0:T(128)S(1)}, s32[4]{0:T(128)}, u32[]{:S(2)}) copy-start(s32[4]{0:T(128)} %param.26) | copy-start | bytes 52
  167.4 3.1 copy-start.14
  167.4 3.1 copy-start.15
  170.5 9.2 %slice-start = ((s8[6291456]{0:T(1024)(128)(4,1)}), s8[4194304]{0:T(1024)(128)(4,1)S(1)}, s32[]{:S(2)}) async-start(s8[6291456]{0:T(1024)(128)(4,1)} %bitcast.113), calls=%async_computation.9 | async-start | bytes 8388608
  171.9 6.9 %copy-start.11 = (bf16[4,4,16,112]{3,1,0,2:T(4,128)(2,1)}, bf16[4,4,16,112]{3,1,0,2:T(4,128)(2,1)S(1)}, u32[]{:S(2)}) copy-start(bf16[4,4,16,112]{3,1,0,2:T(4,128)(2,1)S(1)} %get-tuple-element.269) | copy-start | bytes 172036
  171.9 7.8 %slice-start.1 = ((s8[6291456]{0:T(1024)(128)(4,1)}), s8[2097152]{0:T(1024)(128)(4,1)S(1)}, s32[]{:S(2)}) async-start(s8[6291456]{0:T(1024)(128)(4,1)} %bitcast.113), calls=%async_computation.10 | async-start | bytes 4194304
  171.9 7.8 %copy-start.19 = (pred[4,768]{1,0:T(4,128)(4,1)S(1)}, pred[4,768]{1,0:T(4,128)(4,1)}, u32[]{:S(2)}) copy-start(pred[4,768]{1,0:T(4,128)(4,1)} %fusion.54) | copy-start | bytes 9220
  178.8 0.9 copy-start.9
  184.3 55.7 %copy-start.10 = (bf16[16,3584]{1,0:T(8,128)(2,1)S(1)}, bf16[16,3584]{1,0:T(8,128)(2,1)}, u32[]{:S(2)}) copy-start(bf16[16,3584]{1,0:T(8,128)(2,1)} %get-tuple-element.255) | copy-start | bytes 344068
  184.3 172.4 %all-reduce.7.cloned.1.call-start = ((), (), s32[]{:S(2)}) async-start(), calls=%async_computation.5 | async-start | bytes 917504 | tf_op jit(solution)/shard_map/psum | solution.py:169
  211.7 23.1 %copy-start.12 = (f32[64,4,16]{2,1,0:T(4,128)}, f32[64,4,16]{2,1,0:T(4,128)S(1)}, u32[]{:S(2)}) copy-start(f32[64,4,16]{2,1,0:T(4,128)S(1)} %all-gather.1) | copy-start | bytes 49156
  233.6 1.2 copy-start.13
  274.0 1.4 copy-start.18
  274.0 82.7 %copy-start.4 = (bf16[16,3584]{1,0:T(8,128)(2,1)S(1)}, bf16[16,3584]{1,0:T(8,128)(2,1)}, u32[]{:S(2)}) copy-start(bf16[16,3584]{1,0:T(8,128)(2,1)} %copy-done.3) | copy-start | bytes 344068
  274.1 82.7 %copy-start.8 = (bf16[16,3584]{1,0:T(8,128)(2,1)S(1)}, bf16[16,3584]{1,0:T(8,128)(2,1)}, u32[]{:S(2)}) copy-start(bf16[16,3584]{1,0:T(8,128)(2,1)} %param.20) | copy-start | bytes 344068
  275.4 156.4 %all-reduce.11.cloned.1.call-start = ((), (), s32[]{:S(2)}) async-start(), calls=%async_computation.8 | async-start | bytes 1835008 | tf_op jit(solution)/shard_map/psum | solution.py:176
  356.7 12.9 %copy-start.5 = (bf16[896,896]{1,0:T(8,128)(2,1)S(1)}, bf16[896,896]{1,0:T(8,128)(2,1)}, u32[]{:S(2)}) copy-start(bf16[896,896]{1,0:T(8,128)(2,1)} %param.30) | copy-start | bytes 4816900
  358.1 12.9 %copy-start.1 = (bf16[16,7168]{1,0:T(8,128)(2,1)}, bf16[16,7168]{1,0:T(8,128)(2,1)S(1)}, u32[]{:S(2)}) copy-start(bf16[16,7168]{1,0:T(8,128)(2,1)S(1)} %get-tuple-element.249) | copy-start | bytes 688132
  358.1 12.8 %copy-start.6 = (bf16[896,896]{1,0:T(8,128)(2,1)S(1)}, bf16[896,896]{1,0:T(8,128)(2,1)}, u32[]{:S(2)}) copy-start(bf16[896,896]{1,0:T(8,128)(2,1)} %param.31) | copy-start | bytes 4816900
  372.2 148.9 %all-reduce.9.cloned.1.call-start = ((), (), s32[]{:S(2)}) async-start(), calls=%async_computation.7 | async-start | bytes 917504
  433.9 3.2 copy-start.2
  433.9 7.3 %copy-start.22 = (u32[128]{0:T(128)S(1)}, u32[128]{0:T(128)}, u32[]{:S(2)}) copy-start(u32[128]{0:T(128)} %constant.127) | copy-start | bytes 1540
  437.9 10.5 %all-to-all-start.1 = ((bf16[16,8,896]{2,0,1:T(8,128)(2,1)}), bf16[16,8,896]{2,0,1:T(8,128)(2,1)S(1)}, u32[]{:S(2)}, u32[]{:S(2)}) async-start(bf16[16,8,896]{2,0,1:T(8,128)(2,1)} %bitcast.123), calls=%async_computation.2 | async-start | bytes 458752 | tf_op jit(solution)/shard_map/all_to_all | solution.py:173
Sparse Core Ops, SparseCore 0:
  109.4 29.5 reduce-scatter.1
  184.4 48.8 all-gather.5
  275.5 81.1 all-reduce.6
  372.3 59.4 all-reduce.10
  437.3 83.7 all-reduce.8
where the time goes:
time: 532 us; the launch traced here: 529 us
  waiting for transfers between devices  195 us (37%)
  blocking collectives  179 us (34%)
  local copies, waits for them, and re-layouts  66.7 us (13%)
  other arithmetic  40.1 us (8%)
  matrix products  26 us (5%)
  between operations  14.2 us (3%)
  starting transfers between devices  7.46 us (1%)
    psum x1, waiting for transfers between devices, body(): mixed_sum = lax.psum(projected_out, 'seq')  81.3 us
    psum x1, blocking collectives, body(): everywhere = lax.psum(looked, ('seq', 'req'))  74.1 us
    unnamed x6, waiting for transfers between devices  72.8 us
    all_gather x2, blocking collectives, merged_2(): everything = jax.tree.map(lambda part: lax.all_gather(part, axis), array)  44.8 us
    psum x1, waiting for transfers between devices, body(): lax.psum((jnp.dot(second_spread_state, gate_weight, preferred_element_typ...  34.2 us
    all_gather x1, blocking collectives, body(): lax.all_gather(qkv_part.astype(jnp.bfloat16), 'seq', axis=1, tiled=True)  24.2 us
    psum x1, blocking collectives, body(): lax.psum((jnp.dot(second_spread_state, gate_weight, preferred_element_typ...  24.2 us
    dynamic_slice x15, local copies, waits for them, and re-layouts, hop(): return combine(so_far, jax.tree.map(lambda part: part[k], everything))  14.7 us
  transfers between devices with their start and end apart: 7, of which 5 were waited for; matrix products, arithmetic and copies ran while one was open for 10% of the time, Pallas kernels for 0%

commit v1 on v0

--- a/solution.py
+++ b/solution.py
@@ -88,7 +88,9 @@
         jnp.float32
     )
     looked = jnp.where(present[:, None], looked, 0.0)
-    everywhere = lax.psum(looked, ("seq", "req"))
+    everywhere = looked
+    for mesh_axis in ("req", "seq"):
+        everywhere = lax.psum(everywhere, mesh_axis)
     embedded = lax.dynamic_slice_in_dim(everywhere, req_index * group_rows, group_rows, 0)
     joined = jnp.concatenate([hidden, embedded.astype(jnp.bfloat16)], axis=1)
     normed = rms_norm(joined, attention_norm_gain)

time: 532 us -> 609 us (1.14)
  waiting for transfers between devices: 195 us -> 264 us
  blocking collectives: 179 us -> 192 us
    psum x0 -> x1, waiting for transfers between devices: none -> 64.2 us  [body(): everywhere = lax.psum(everywhere, mesh_axis)]
    psum x1, blocking collectives: 74.1 us -> 89.7 us  [body(): everywhere = lax.psum(everywhere, mesh_axis)]
    unnamed x6 -> x7, waiting for transfers between devices: 72.8 us -> 72.8 us
  transfers between devices with their start and end apart: 7 -> 8, of which waited for: 5 -> 6; matrix products, arithmetic and copies ran while one was open for 10% -> 8% of each run, Pallas kernels for 0% -> 0%
where the time goes in v1:
time: 609 us; the launch traced here: 606 us
  waiting for transfers between devices  264 us (43%)
  blocking collectives  192 us (32%)
  local copies, waits for them, and re-layouts  64.9 us (11%)
  other arithmetic  36.2 us (6%)
  matrix products  26.1 us (4%)
  between operations  14.5 us (2%)
  starting transfers between devices  7.31 us (1%)
    psum x1, blocking collectives, body(): everywhere = lax.psum(everywhere, mesh_axis)  89.7 us
    psum x1, waiting for transfers between devices, body(): mixed_sum = lax.psum(projected_out, 'seq')  81.5 us
    unnamed x7, waiting for transfers between devices  72.8 us
    psum x1, waiting for transfers between devices, body(): everywhere = lax.psum(everywhere, mesh_axis)  64.2 us
    all_gather x2, blocking collectives, merged_2(): everything = jax.tree.map(lambda part: lax.all_gather(part, axis), array)  44.8 us
    psum x1, waiting for transfers between devices, body(): lax.psum((jnp.dot(second_spread_state, gate_weight, preferred_element_typ...  34.2 us
    psum x1, blocking collectives, body(): lax.psum((jnp.dot(second_spread_state, gate_weight, preferred_element_typ...  24.2 us
    all_gather x1, blocking collectives, body(): lax.all_gather(qkv_part.astype(jnp.bfloat16), 'seq', axis=1, tiled=True)  22.2 us
  transfers between devices with their start and end apart: 8, of which 6 were waited for; matrix products, arithmetic and copies ran while one was open for 8% of the time, Pallas kernels for 0%

profile of v1, /device:TPU:0, one launch (start us, length us, event | category | flops | bytes accessed | tf_op | source)
XLA Modules:
  0.0 606.2 jit_solution(9105816548370793050)
XLA Ops:
  7.4 4.9 gather_fusion
  12.2 2.8 convert_select_fusion
  18.3 64.2 %all-reduce.8.cloned.1.call-done = f32[128,3584]{1,0:T(8,128)} async-done(((f32[128,3584]{1,0:T(8,128)}), f32[128,3584]{1,0:T(8,128)}) %all-reduce.8.cloned.1.call-update) | async-done | bytes 1835024 | tf_op jit(solution)/shard_map/psum | solution.py:93
  82.5 89.7 %all-reduce.15 = bf16[128,3584]{1,0:T(8,128)(2,1)} all-reduce(f32[128,3584]{1,0:T(8,128)} %all-reduce.8.cloned.1.call-done), channel_id=1, replica_groups=mesh['seq'=16,'req'=8] {'seq'}, use_global_device_ids=true, to_apply=%region_1.2 | all-reduce | flops 458752 | bytes 2752512 | tf_op jit(solution)/shard_map/psum | solution.py:93
  175.8 3.7 all-to-all-start
  179.5 1.3 add_convert_fusion.2
  180.9 5.8 all-to-all-done
  186.7 2.6 fusion.67
  190.1 13.2 %reshape.185 = bf16[768,16,224]{2,1,0:T(8,128)(2,1)} reshape(bf16[6,1,128,3584]{3,2,1,0:T(8,128)(2,1)} %param.24) | data formatting | bytes 11010048 | tf_op jit(solution)/shard_map/reshape | solution.py:115
  203.3 13.1 %reshape.186 = bf16[768,16,224]{2,1,0:T(8,128)(2,1)} reshape(bf16[6,1,128,3584]{3,2,1,0:T(8,128)(2,1)} %param.25) | data formatting | bytes 11010048 | tf_op jit(solution)/shard_map/reshape | solution.py:116
  218.7 22.2 %all-gather.3 = bf16[16,672,16]{1,2,0:T(8,128)(2,1)S(1)} all-gather(bf16[1,672,16]{1,2,0:T(8,128)(2,1)S(1)} %convert_bitcast_fusion), channel_id=1, replica_groups=mesh['seq'=16,'req'=8] {'seq'}, dimensions={0}, use_global_device_ids=true | all-gather | bytes 365568 | tf_op jit(solution)/shard_map/all_gather | solution.py:105
  241.8 1.5 reshape.211
  247.4 1.3 subtract_convert_fusion
  248.8 6.8 %select_reduce_fusion = (f32[4,4,16]{1,0,2:T(4,128)S(1)}, f32[4,4,16,768]{3,1,0,2:T(4,128)S(1)}) fusion(pred[4,768]{1,0:T(4,128)(4,1)} %fusion.54, bf16[768,16,224,1]{2,1,0,3:T(8,128)(2,1)} %bitcast.116, bf16[4,4,16,112]{3,1,0,2:T(4,128)(2,1)S(1)} %get-tuple-element.268, bf16[4,4,16,112]{3,1,0,2:T(4,128)(2,1)S(1)} %get-tuple-element.269), kind=kOutput, calls=%fused_computation.25 | convolution fusion | flops 88899328 | bytes 6410240 | tf_op jit(solution)/shard_map/rthd,khd->rthk/dot_general | solution.py:131
  256.5 4.6 fusion.16
  262.4 2.3 fusion.21
  265.5 22.9 %all-gather.1 = f32[64,4,16]{2,1,0:T(4,128)S(1)} all-gather(f32[4,4,16]{2,1,0:T(4,128)S(1)} %copy.119), channel_id=3, replica_groups=mesh['seq'=16,'req'=8] {'seq'}, dimensions={0}, use_global_device_ids=true | all-gather | bytes 17408 | tf_op jit(solution)/shard_map/all_gather | solution.py:15
  288.4 21.9 %all-gather = f32[64,4,16]{2,1,0:T(4,128)S(1)} all-gather(f32[4,4,16]{2,1,0:T(4,128)} %copy.118), channel_id=2, replica_groups=mesh['seq'=16,'req'=8] {'seq'}, dimensions={0}, use_global_device_ids=true | all-gather | bytes 17408 | tf_op jit(solution)/shard_map/all_gather | solution.py:15
  318.9 29.8 %while.19 = (s32[]{:T(128)}, f32[4,4,16]{2,1,0:T(4,128)S(1)}, f32[4,4,16]{2,1,0:T(4,128)S(1)}, f32[4,4,16,224]{3,2,1,0:T(8,128)S(1)}, f32[16,4,4,16]{3,2,1,0:T(4...) while((s32[]{:T(128)}, f32[4,4,16]{2,1,0:T(4,128)S(1)}, ...), condition=%wide.region_9.10_spmd, body=%wide.region_8.9_spmd.sunk | while | flops 173573 | bytes 1157271 | solution.py:21
  350.7 1.3 fusion.68
  352.1 81.5 %all-reduce.10.cloned.1.call-done = f32[16,7168]{1,0:T(8,128)} async-done(((f32[16,7168]{1,0:T(8,128)}), f32[16,7168]{1,0:T(8,128)}) %all-reduce.10.cloned.1.call-update) | async-done | bytes 458768 | tf_op jit(solution)/shard_map/psum | solution.py:171
  433.6 1.3 fusion.24
  435.1 11.4 %all_to_all.54 = bf16[16,8,896]{2,0,1:T(8,128)(2,1)S(1)} all-to-all(bf16[16,8,896]{2,0,1:T(8,128)(2,1)S(1)} %bitcast.125), channel_id=1, replica_groups=mesh['seq'=16,'req'=8] {'req'}, dimensions={1} | all-to-all | bytes 458752 | tf_op jit(solution)/shard_map/all_to_all | solution.py:176
  447.8 1.3 fusion.71
  450.3 24.2 %psum.46 = bf16[128,128]{1,0:T(8,128)(2,1)S(1)} all-reduce(f32[128,128]{1,0:T(8,128)S(1)} %fusion.70), channel_id=1, replica_groups=mesh['seq'=16,'req'=8] {'req'}, use_global_device_ids=true, to_apply=%region_15.16 | all-reduce | flops 16384 | bytes 98304 | tf_op jit(solution)/shard_map/psum | solution.py:178
  474.4 34.2 %all-reduce.14.cloned.1.call-done = (f32[128,896]{1,0:T(8,128)}, f32[128,896]{1,0:T(8,128)}) async-done(((f32[128,896]{1,0:T(8,128)}, f32[128,896]{1,0:T(8,128)}), (f32[128,896]{1,0:T(8,128)}, f32[128,896]{1,0:T(8,128)})) %all-reduce.14.cloned.1.call-update) | async-done | bytes 917520 | tf_op jit(solution)/shard_map/psum | solution.py:178
  508.7 2.2 convolution_add_fusion.1
  510.8 3.2 fusion.19
  514.8 3.4 all-to-all-start.1
  519.4 5.9 all-to-all-done.1
  525.3 72.7 %all-reduce.12.cloned.1.call-done = f32[128,896]{1,0:T(8,128)} async-done(((f32[128,896]{1,0:T(8,128)}), f32[128,896]{1,0:T(8,128)}) %all-reduce.12.cloned.1.call-update) | async-done | bytes 458768
  598.0 1.4 fusion.45
  (180 shorter events, 62.6 us)
Async XLA Ops:
  6.5 344.1 %copy-start = (bf16[224,7168]{1,0:T(8,128)(2,1)S(1)}, bf16[224,7168]{1,0:T(8,128)(2,1)}, u32[]{:S(2)}) copy-start(bf16[224,7168]{1,0:T(8,128)(2,1)} %param.28) | copy-start | bytes 9633796
  6.5 76.0 %all-reduce.8.cloned.1.call-start = ((), (), s32[]{:S(2)}) async-start(), calls=%async_computation.4 | async-start | bytes 3670016 | tf_op jit(solution)/shard_map/psum | solution.py:93
  12.2 2.9 copy-start.7
  12.2 2.9 copy-start.18
  12.2 3.6 copy-start.22
  173.2 16.1 %copy-start.3 = (bf16[16,3584]{1,0:T(8,128)(2,1)}, bf16[16,3584]{1,0:T(8,128)(2,1)S(1)}, u32[]{:S(2)}) copy-start(bf16[16,3584]{1,0:T(8,128)(2,1)S(1)} %dynamic-slice_convert_fusion) | copy-start | bytes 344068
  175.8 10.9 %all-to-all-start = ((bf16[16,8,896]{2,0,1:T(8,128)(2,1)}), bf16[16,8,896]{2,0,1:T(8,128)(2,1)S(1)}, u32[]{:S(2)}, u32[]{:S(2)}) async-start(bf16[16,8,896]{2,0,1:T(8,128)(2,1)} %copy.113), calls=%async_computation | async-start | bytes 458752 | tf_op jit(solution)/shard_map/all_to_all | solution.py:97
  179.5 38.4 %reduce-scatter.2.cloned.1.call-start = ((), (), s32[]{:S(2)}) async-start(), calls=%async_computation.5 | async-start | bytes 442368 | tf_op jit(solution)/shard_map/reduce_scatter | solution.py:99
  189.3 128.5 %all-gather.6.cloned.1.call-start = ((), (), s32[]{:S(2)}) async-start(), calls=%async_computation.7 | async-start | bytes 4456448 | tf_op jit(solution)/shard_map/all_gather | solution.py:15
  203.3 13.2 %copy-start.21 = (f32[4,4]{1,0:T(4,128)S(1)}, f32[4,4]{1,0:T(4,128)}, u32[]{:S(2)}) copy-start(f32[4,4]{1,0:T(4,128)} %add_convert_fusion.2) | copy-start | bytes 196
  203.3 14.0 %copy-start.16 = (s32[768]{0:T(1024)S(1)}, s32[768]{0:T(1024)}, u32[]{:S(2)}) copy-start(s32[768]{0:T(1024)} %iota_bitcast_fusion) | copy-start | bytes 9220
  203.3 14.0 %copy-start.17 = (pred[1,4,6,128]{3,2,1,0:T(8,128)(4,1)S(1)}, pred[1,4,6,128]{3,2,1,0:T(8,128)(4,1)}, u32[]{:S(2)}) copy-start(pred[1,4,6,128]{3,2,1,0:T(8,128)(4,1)} %broadcast_bitcast_fusion.1) | copy-start | bytes 9220
  203.3 14.0 %copy-start.24 = (s32[4]{0:T(128)S(1)}, s32[4]{0:T(128)}, u32[]{:S(2)}) copy-start(s32[4]{0:T(128)} %param.26) | copy-start | bytes 52
  244.2 3.1 copy-start.14
  244.2 3.1 copy-start.15
  247.4 9.1 %slice-start = ((s8[6291456]{0:T(1024)(128)(4,1)}), s8[4194304]{0:T(1024)(128)(4,1)S(1)}, s32[]{:S(2)}) async-start(s8[6291456]{0:T(1024)(128)(4,1)} %bitcast.113), calls=%async_computation.10 | async-start | bytes 8388608
  248.7 6.9 %copy-start.11 = (bf16[4,4,16,112]{3,1,0,2:T(4,128)(2,1)}, bf16[4,4,16,112]{3,1,0,2:T(4,128)(2,1)S(1)}, u32[]{:S(2)}) copy-start(bf16[4,4,16,112]{3,1,0,2:T(4,128)(2,1)S(1)} %get-tuple-element.269) | copy-start | bytes 172036
  248.7 7.8 %slice-start.1 = ((s8[6291456]{0:T(1024)(128)(4,1)}), s8[2097152]{0:T(1024)(128)(4,1)S(1)}, s32[]{:S(2)}) async-start(s8[6291456]{0:T(1024)(128)(4,1)} %bitcast.113), calls=%async_computation.11 | async-start | bytes 4194304
  248.7 7.8 %copy-start.20 = (pred[4,768]{1,0:T(4,128)(4,1)S(1)}, pred[4,768]{1,0:T(4,128)(4,1)}, u32[]{:S(2)}) copy-start(pred[4,768]{1,0:T(4,128)(4,1)} %fusion.54) | copy-start | bytes 9220
  261.1 55.5 %copy-start.10 = (bf16[16,3584]{1,0:T(8,128)(2,1)S(1)}, bf16[16,3584]{1,0:T(8,128)(2,1)}, u32[]{:S(2)}) copy-start(bf16[16,3584]{1,0:T(8,128)(2,1)} %get-tuple-element.255) | copy-start | bytes 344068
  261.1 172.4 %all-reduce.10.cloned.1.call-start = ((), (), s32[]{:S(2)}) async-start(), calls=%async_computation.6 | async-start | bytes 917504 | tf_op jit(solution)/shard_map/psum | solution.py:171
  288.4 23.1 %copy-start.12 = (f32[64,4,16]{2,1,0:T(4,128)}, f32[64,4,16]{2,1,0:T(4,128)S(1)}, u32[]{:S(2)}) copy-start(f32[64,4,16]{2,1,0:T(4,128)S(1)} %all-gather.1) | copy-start | bytes 49156
  350.7 82.9 %copy-start.4 = (bf16[16,3584]{1,0:T(8,128)(2,1)S(1)}, bf16[16,3584]{1,0:T(8,128)(2,1)}, u32[]{:S(2)}) copy-start(bf16[16,3584]{1,0:T(8,128)(2,1)} %copy-done.3) | copy-start | bytes 344068
  350.7 82.9 %copy-start.8 = (bf16[16,3584]{1,0:T(8,128)(2,1)S(1)}, bf16[16,3584]{1,0:T(8,128)(2,1)}, u32[]{:S(2)}) copy-start(bf16[16,3584]{1,0:T(8,128)(2,1)} %param.20) | copy-start | bytes 344068
  352.0 156.6 %all-reduce.14.cloned.1.call-start = ((), (), s32[]{:S(2)}) async-start(), calls=%async_computation.9 | async-start | bytes 1835008 | tf_op jit(solution)/shard_map/psum | solution.py:178
  433.6 12.9 %copy-start.5 = (bf16[896,896]{1,0:T(8,128)(2,1)S(1)}, bf16[896,896]{1,0:T(8,128)(2,1)}, u32[]{:S(2)}) copy-start(bf16[896,896]{1,0:T(8,128)(2,1)} %param.30) | copy-start | bytes 4816900
  434.9 12.9 %copy-start.1 = (bf16[16,7168]{1,0:T(8,128)(2,1)}, bf16[16,7168]{1,0:T(8,128)(2,1)S(1)}, u32[]{:S(2)}) copy-start(bf16[16,7168]{1,0:T(8,128)(2,1)S(1)} %get-tuple-element.249) | copy-start | bytes 688132
  434.9 12.8 %copy-start.6 = (bf16[896,896]{1,0:T(8,128)(2,1)S(1)}, bf16[896,896]{1,0:T(8,128)(2,1)}, u32[]{:S(2)}) copy-start(bf16[896,896]{1,0:T(8,128)(2,1)} %param.31) | copy-start | bytes 4816900
  449.1 148.9 %all-reduce.12.cloned.1.call-start = ((), (), s32[]{:S(2)}) async-start(), calls=%async_computation.8 | async-start | bytes 917504
  510.8 3.2 copy-start.2
  510.8 7.4 %copy-start.25 = (u32[128]{0:T(128)S(1)}, u32[128]{0:T(128)}, u32[]{:S(2)}) copy-start(u32[128]{0:T(128)} %constant.127) | copy-start | bytes 1540
  514.8 10.5 %all-to-all-start.1 = ((bf16[16,8,896]{2,0,1:T(8,128)(2,1)}), bf16[16,8,896]{2,0,1:T(8,128)(2,1)S(1)}, u32[]{:S(2)}, u32[]{:S(2)}) async-start(bf16[16,8,896]{2,0,1:T(8,128)(2,1)} %bitcast.123), calls=%async_computation.2 | async-start | bytes 458752 | tf_op jit(solution)/shard_map/all_to_all | solution.py:175
  (4 other events, 6.3 us)
Sparse Core Ops, SparseCore 0:
  15.2 67.3 all-reduce.7
  189.4 26.3 reduce-scatter.1
  261.3 48.9 all-gather.5
  352.1 81.3 all-reduce.9
  449.2 59.4 all-reduce.13
  514.2 83.7 all-reduce.11
